TPU v7x, 256 devices: a whole 4x4x8 slice. The times are simulated.
256 devices in a mesh: dp: 64 (over z, y, x_hi), seq: 4 (over x_lo, core).
Axes of the slice: x: 4 (x_hi: 2, x_lo: 2; x = x_hi * 2 + x_lo), y: 4, z: 8, core: 2. Of those that a mesh axis runs over, the one named last changes fastest.
Arguments:
- queries: bfloat16 [32768, 2560], P(('dp', 'seq')), may hold values from -400 to 400
- key_states: bfloat16 [32768, 2560], P(('dp', 'seq')), may hold values from -400 to 400
- value_states: bfloat16 [32768, 2560], P(('dp', 'seq')), may hold values from -6 to 6
- query_tangent: bfloat16 [32768, 2560], P(('dp', 'seq')), may hold values from -6 to 6
- key_tangent: bfloat16 [32768, 2560], P(('dp', 'seq')), may hold values from -6 to 6
- value_tangent: bfloat16 [32768, 2560], P(('dp', 'seq')), may hold values from -6 to 6
- query_gain: float32 [2560], replicated, may hold values from 0.25 to 1.75
- key_gain: float32 [2560], replicated, may hold values from 0.25 to 1.75
- out_weight: bfloat16 [2560, 5120], P('seq', 'dp'), may hold values from -0.125 to 0.125
Outputs:
- projected: bfloat16 [32768, 5120], P(('dp', 'seq'))
- projected_tangent: bfloat16 [32768, 5120], P(('dp', 'seq'))
All inputs are finite; a program needn't handle non-finite values.
Results may differ from a plain program's by a relative error of at most 0.012.
The roundings to bfloat16 on the way count: a program that leaves them out, or rounds other values in their place, can miss the bound.
Values may be sent and summed in bfloat16 or wider, within the bound.
A program may use at most 128 MiB of HBM per device.

v0:
```python
import jax
import jax.numpy as jnp
from jax import lax
from jax.sharding import PartitionSpec as P

HEADS = 20
HDIM = 128


def rms_tangent(primal, tangent, gain):
    primal_f = primal.astype(jnp.float32)
    tangent_f = tangent.astype(jnp.float32)
    inverse = lax.rsqrt(jnp.mean(primal_f * primal_f, axis=-1, keepdims=True) + 1e-06)
    across = jnp.mean(primal_f * tangent_f, axis=-1, keepdims=True)
    normed = (primal_f * inverse * gain).astype(jnp.bfloat16)
    normed_tangent = (gain * (tangent_f * inverse - primal_f * inverse**3 * across)).astype(
        jnp.bfloat16
    )
    return (normed, normed_tangent)


def attend(query_normed, query_dual, key_normed, key_dual, value_plain, value_dual):
    factor = HDIM ** (-0.5)
    scores = (
        jnp.einsum("qhd,khd->hqk", query_normed, key_normed, preferred_element_type=jnp.float32)
        * factor
    )
    dual_scores = (
        jnp.einsum("qhd,khd->hqk", query_dual, key_normed, preferred_element_type=jnp.float32)
        + jnp.einsum("qhd,khd->hqk", query_normed, key_dual, preferred_element_type=jnp.float32)
    ) * factor
    peak = jnp.max(scores, axis=-1, keepdims=True)
    raised = jnp.exp(scores - peak)
    probs = raised / jnp.sum(raised, axis=-1, keepdims=True)
    spread = probs * (dual_scores - jnp.sum(probs * dual_scores, axis=-1, keepdims=True))
    probs_low = probs.astype(jnp.bfloat16)
    spread_low = spread.astype(jnp.bfloat16)
    attn = jnp.einsum(
        "hqk,khd->qhd", probs_low, value_plain, preferred_element_type=jnp.float32
    ).astype(jnp.bfloat16)
    dual_attn = (
        jnp.einsum("hqk,khd->qhd", probs_low, value_dual, preferred_element_type=jnp.float32)
        + jnp.einsum("hqk,khd->qhd", spread_low, value_plain, preferred_element_type=jnp.float32)
    ).astype(jnp.bfloat16)
    return (attn, dual_attn)


def body(
    queries,
    key_states,
    value_states,
    query_tangent,
    key_tangent,
    value_tangent,
    query_gain,
    key_gain,
    out_weight,
):
    rows_here = queries.shape[0]
    query_normed, query_dual = rms_tangent(queries, query_tangent, query_gain)
    key_normed, key_dual = rms_tangent(key_states, key_tangent, key_gain)
    by_head = (
        lax.all_to_all(
            query_normed.reshape(rows_here, HEADS, HDIM),
            "seq",
            split_axis=1,
            concat_axis=0,
            tiled=True,
        ),
        lax.all_to_all(
            query_dual.reshape(rows_here, HEADS, HDIM),
            "seq",
            split_axis=1,
            concat_axis=0,
            tiled=True,
        ),
        lax.all_to_all(
            key_normed.reshape(rows_here, HEADS, HDIM),
            "seq",
            split_axis=1,
            concat_axis=0,
            tiled=True,
        ),
        lax.all_to_all(
            key_dual.reshape(rows_here, HEADS, HDIM), "seq", split_axis=1, concat_axis=0, tiled=True
        ),
        lax.all_to_all(
            value_states.reshape(rows_here, HEADS, HDIM),
            "seq",
            split_axis=1,
            concat_axis=0,
            tiled=True,
        ),
        lax.all_to_all(
            value_tangent.reshape(rows_here, HEADS, HDIM),
            "seq",
            split_axis=1,
            concat_axis=0,
            tiled=True,
        ),
    )
    attn, dual_attn = attend(by_head[0], by_head[1], by_head[2], by_head[3], by_head[4], by_head[5])
    width_all = HEADS * HDIM
    back_plain, back_dual = (
        lax.all_to_all(attn, "seq", split_axis=0, concat_axis=1, tiled=True),
        lax.all_to_all(dual_attn, "seq", split_axis=0, concat_axis=1, tiled=True),
    )
    stacked = jnp.concatenate(
        [back_plain.reshape(rows_here, width_all), back_dual.reshape(rows_here, width_all)], axis=0
    )
    full_rows = lax.all_gather(out_weight, "seq", axis=0, tiled=True)
    result = jnp.dot(
        stacked,
        lax.all_gather(full_rows, "dp", axis=1, tiled=True),
        preferred_element_type=jnp.float32,
    ).astype(jnp.bfloat16)
    return (result[:rows_here], result[rows_here:])


def solution(mesh):
    return jax.shard_map(
        body,
        mesh=mesh,
        in_specs=(
            P(("dp", "seq"), None),
            P(("dp", "seq"), None),
            P(("dp", "seq"), None),
            P(("dp", "seq"), None),
            P(("dp", "seq"), None),
            P(("dp", "seq"), None),
            P(),
            P(),
            P("seq", "dp"),
        ),
        out_specs=(P(("dp", "seq"), None), P(("dp", "seq"), None)),
        check_vma=False,
    )
```

profile of v0, /device:TPU:24, one launch (start us, length us, event | category | flops | bytes accessed | tf_op | source)
XLA Modules:
  0.0 334.1 jit_solution(1563490094878376542)
XLA Ops:
  7.2 8.2 %all_gather.6 = bf16[2560,80]{0,1:T(8,128)(2,1)} all-gather(bf16[640,80]{0,1:T(8,128)(2,1)} %param.17), channel_id=1, replica_groups=mesh['dp'=64,'seq'=4] {'seq'}, dimensions={0}, use_global_device_ids=true | all-gather | bytes 512000 | tf_op jit(solution)/shard_map/all_gather | solution.py:111
  15.5 1.4 copy.63
  16.9 0.3 copy.80
  17.3 0.4 fusion.24
  17.7 1.6 fusion.14
  19.3 3.6 %all-to-all-start.1 = ((bf16[128,20,128]{0,2,1:T(8,128)(2,1)}), bf16[128,20,128]{0,2,1:T(8,128)(2,1)S(1)}, u32[]{:S(2)}, u32[]{:S(2)}) async-start(bf16[128,20,128]{0,2,1:T(8,128)(2,1)} %bitcast.5), calls=%async_computation.1 | async-start | bytes 1310720 | tf_op jit(solution)/shard_map/all_to_all | solution.py:77
  22.9 0.3 copy.60
  23.3 0.3 copy.77
  23.6 0.4 fusion.19
  24.0 1.4 fusion.11
  25.4 7.7 %all-to-all-done.1 = bf16[128,20,128]{0,2,1:T(8,128)(2,1)S(1)} async-done(((bf16[128,20,128]{0,2,1:T(8,128)(2,1)}), bf16[128,20,128]{0,2,1:T(8,128)(2,1)S(1)}, u32[]{:S(2)}, u32[]{:S(2)}) %all-to-all-start.1) | async-done | bytes 655392 | tf_op jit(solution)/shard_map/all_to_all | solution.py:77
  33.1 3.5 %all-to-all-start = ((bf16[128,20,128]{0,2,1:T(8,128)(2,1)}), bf16[128,20,128]{0,2,1:T(8,128)(2,1)S(1)}, u32[]{:S(2)}, u32[]{:S(2)}) async-start(bf16[128,20,128]{0,2,1:T(8,128)(2,1)} %bitcast.68), calls=%async_computation | async-start | bytes 1310720 | tf_op jit(solution)/shard_map/all_to_all | solution.py:63
  36.6 1.4 copy.66
  38.0 8.8 %all-to-all-done = bf16[128,20,128]{0,2,1:T(8,128)(2,1)S(1)} async-done(((bf16[128,20,128]{0,2,1:T(8,128)(2,1)}), bf16[128,20,128]{0,2,1:T(8,128)(2,1)S(1)}, u32[]{:S(2)}, u32[]{:S(2)}) %all-to-all-start) | async-done | bytes 655392 | tf_op jit(solution)/shard_map/all_to_all | solution.py:63
  46.8 13.3 %all_to_all.138 = bf16[128,20,128]{0,2,1:T(8,128)(2,1)} all-to-all(bf16[128,20,128]{0,2,1:T(8,128)(2,1)S(1)} %bitcast.65), channel_id=1, replica_groups=mesh['dp'=64,'seq'=4] {'seq'}, dimensions={1} | all-to-all | bytes 1310720 | tf_op jit(solution)/shard_map/all_to_all | solution.py:87
  60.1 13.4 %all_to_all.139 = bf16[128,20,128]{0,2,1:T(8,128)(2,1)S(1)} all-to-all(bf16[128,20,128]{0,2,1:T(8,128)(2,1)S(1)} %bitcast.67), channel_id=1, replica_groups=mesh['dp'=64,'seq'=4] {'seq'}, dimensions={1} | all-to-all | bytes 1310720 | tf_op jit(solution)/shard_map/all_to_all | solution.py:70
  73.5 3.5 %all-to-all-start.6 = ((bf16[128,20,128]{0,2,1:T(8,128)(2,1)}), bf16[128,20,128]{0,2,1:T(8,128)(2,1)S(1)}, u32[]{:S(2)}, u32[]{:S(2)}) async-start(bf16[128,20,128]{0,2,1:T(8,128)(2,1)} %bitcast.66), calls=%async_computation.6 | async-start | bytes 1310720 | tf_op jit(solution)/shard_map/all_to_all | solution.py:84
  76.9 2.2 copy.73
  79.1 0.3 copy.65
  79.5 0.3 copy.62
  79.8 1.6 copy.68
  81.5 4.1 %fusion.40 = (f32[5,512]{1,0:T(8,128)S(1)}, f32[5,512,512]{1,2,0:T(8,128)}) fusion(bf16[512,5,128]{2,0,1:T(8,128)(2,1)S(1)} %bitcast.71, bf16[512,5,128]{2,0,1:T(8,128)(2,1)S(1)} %bitcast.56), kind=kOutput, calls=%fused_computation.59 | convolution fusion | flops 339476992 | bytes 6563840 | tf_op jit(solution)/shard_map/sub | solution.py:33
  85.6 9.0 %all-to-all-done.6 = bf16[128,20,128]{0,2,1:T(8,128)(2,1)S(1)} async-done(((bf16[128,20,128]{0,2,1:T(8,128)(2,1)}), bf16[128,20,128]{0,2,1:T(8,128)(2,1)S(1)}, u32[]{:S(2)}, u32[]{:S(2)}) %all-to-all-start.6) | async-done | bytes 655392 | tf_op jit(solution)/shard_map/all_to_all | solution.py:84
  94.6 3.5 %all-to-all-start.4 = ((bf16[128,20,128]{0,2,1:T(8,128)(2,1)}), bf16[128,20,128]{0,2,1:T(8,128)(2,1)S(1)}, u32[]{:S(2)}, u32[]{:S(2)}) async-start(bf16[128,20,128]{0,2,1:T(8,128)(2,1)} %bitcast.20), calls=%async_computation.4 | async-start | bytes 1310720 | tf_op jit(solution)/shard_map/all_to_all | solution.py:94
  98.1 3.6 %fusion.32 = bf16[512,5,128]{2,0,1:T(8,128)(2,1)S(1)} fusion(bf16[512,5,128]{2,0,1:T(8,128)(2,1)S(1)} %bitcast.69, f32[5,512,512]{1,2,0:T(8,128)} %get-tuple-element.17, f32[5,512]{1,0:T(8,128)S(1)} %get-tuple-element.16), kind=kOutput, calls=%fused_computation.48 | convolution fusion | flops 338493440 | bytes 6563840 | tf_op jit(solution)/shard_map/hqk,khd->qhd/dot_general | solution.py:38
  101.7 1.4 copy.70
  103.1 0.3 copy.79
  103.4 1.1 copy.82
  104.6 5.5 %all-to-all-done.4 = bf16[128,20,128]{0,2,1:T(8,128)(2,1)S(1)} async-done(((bf16[128,20,128]{0,2,1:T(8,128)(2,1)}), bf16[128,20,128]{0,2,1:T(8,128)(2,1)S(1)}, u32[]{:S(2)}, u32[]{:S(2)}) %all-to-all-start.4) | async-done | bytes 655392 | tf_op jit(solution)/shard_map/all_to_all | solution.py:94
  110.1 3.7 %all-to-all-start.3 = ((bf16[512,5,128]{2,1,0:T(8,128)(2,1)}), bf16[512,5,128]{2,1,0:T(8,128)(2,1)S(1)}, u32[]{:S(2)}, u32[]{:S(2)}) async-start(bf16[512,5,128]{2,1,0:T(8,128)(2,1)} %copy.70), calls=%async_computation.3 | async-start | bytes 2097152 | tf_op jit(solution)/shard_map/all_to_all | solution.py:105
  113.8 1.1 copy.75
  114.9 0.8 fusion.41
  115.7 0.2 copy-done.8
  116.0 1.7 copy-done.11
  117.7 1.0 fusion.28
  118.7 0.1 copy-done.6
  118.8 0.2 copy-done.7
  119.0 1.8 multiply_reduce_fusion
  120.8 1.3 fusion.31
  122.1 1.4 copy.84
  123.6 4.5 %all-to-all-done.3 = bf16[512,5,128]{2,1,0:T(8,128)(2,1)S(1)} async-done(((bf16[512,5,128]{2,1,0:T(8,128)(2,1)}), bf16[512,5,128]{2,1,0:T(8,128)(2,1)S(1)}, u32[]{:S(2)}, u32[]{:S(2)}) %all-to-all-start.3) | async-done | bytes 655392 | tf_op jit(solution)/shard_map/all_to_all | solution.py:105
  128.0 3.5 %all-to-all-start.7 = ((bf16[512,5,128]{2,1,0:T(8,128)(2,1)}), bf16[512,5,128]{2,1,0:T(8,128)(2,1)S(1)}, u32[]{:S(2)}, u32[]{:S(2)}) async-start(bf16[512,5,128]{2,1,0:T(8,128)(2,1)} %copy.84), calls=%async_computation.7 | async-start | bytes 2097152 | tf_op jit(solution)/shard_map/all_to_all | solution.py:106
  131.6 0.6 copy.72
  132.2 13.8 %all-to-all-done.7 = bf16[512,5,128]{2,1,0:T(8,128)(2,1)S(1)} async-done(((bf16[512,5,128]{2,1,0:T(8,128)(2,1)}), bf16[512,5,128]{2,1,0:T(8,128)(2,1)S(1)}, u32[]{:S(2)}, u32[]{:S(2)}) %all-to-all-start.7) | async-done | bytes 655392 | tf_op jit(solution)/shard_map/all_to_all | solution.py:106
  146.0 1.3 copy.86
  147.2 166.1 %all-gather.2.cloned.1.call-done = bf16[2560,5120]{0,1:T(8,128)(2,1)} async-done(((bf16[2560,80]{0,1:T(8,128)(2,1)}), bf16[2560,5120]{0,1:T(8,128)(2,1)}) %all-gather.2.cloned.1.call-update) | async-done | bytes 26214416 | tf_op jit(solution)/shard_map/all_gather | solution.py:114
  313.3 12.3 %convolution_convert_fusion = bf16[256,5120]{1,0:T(8,128)(2,1)S(1)} fusion(bf16[2560,5120]{0,1:T(8,128)(2,1)} %all-gather.2.cloned.1.call-done, bf16[128,2560]{0,1:T(8,128)(2,1)} %bitcast.75, bf16[128,2560]{0,1:T(8,128)(2,1)S(1)} %bitcast.74), kind=kOutput, calls=%fused_computation.1 | convolution fusion | flops 6714818560 | bytes 30146560 | tf_op jit(solution)/shard_map/dot_general | solution.py:112
  325.6 1.7 fusion.39
  (24 shorter events, 0.1 us)
Async XLA Ops:
  7.2 9.7 %copy-start = (bf16[128,2560]{1,0:T(8,128)(2,1)S(1)}, bf16[128,2560]{1,0:T(8,128)(2,1)}, u32[]{:S(2)}) copy-start(bf16[128,2560]{1,0:T(8,128)(2,1)} %param.13) | copy-start | bytes 1966084
  7.2 10.5 %copy-start.9 = (f32[2560]{0:T(1024)S(1)}, f32[2560]{0:T(1024)}, u32[]{:S(2)}) copy-start(f32[2560]{0:T(1024)} %param.16) | copy-start | bytes 30724
  7.2 306.1 %all-gather.2.cloned.1.call-start = ((), (), s32[]{:S(2)}) async-start(), calls=%async_computation.8 | async-start | bytes 26624000 | tf_op jit(solution)/shard_map/all_gather | solution.py:114
  17.2 5.7 %copy-start.1 = (bf16[128,2560]{1,0:T(8,128)(2,1)S(1)}, bf16[128,2560]{1,0:T(8,128)(2,1)}, u32[]{:S(2)}) copy-start(bf16[128,2560]{1,0:T(8,128)(2,1)} %param.9) | copy-start | bytes 1966084
  17.7 5.6 %copy-start.2 = (bf16[128,2560]{1,0:T(8,128)(2,1)S(1)}, bf16[128,2560]{1,0:T(8,128)(2,1)}, u32[]{:S(2)}) copy-start(bf16[128,2560]{1,0:T(8,128)(2,1)} %param.12) | copy-start | bytes 1966084
  19.3 4.7 %copy-start.10 = (f32[2560]{0:T(1024)S(1)}, f32[2560]{0:T(1024)}, u32[]{:S(2)}) copy-start(f32[2560]{0:T(1024)} %param.15) | copy-start | bytes 30724
  19.3 13.8 %all-to-all-start.1 = ((bf16[128,20,128]{0,2,1:T(8,128)(2,1)}), bf16[128,20,128]{0,2,1:T(8,128)(2,1)S(1)}, u32[]{:S(2)}, u32[]{:S(2)}) async-start(bf16[128,20,128]{0,2,1:T(8,128)(2,1)} %bitcast.5), calls=%async_computation.1 | async-start | bytes 1310720 | tf_op jit(solution)/shard_map/all_to_all | solution.py:77
  33.1 13.7 %all-to-all-start = ((bf16[128,20,128]{0,2,1:T(8,128)(2,1)}), bf16[128,20,128]{0,2,1:T(8,128)(2,1)S(1)}, u32[]{:S(2)}, u32[]{:S(2)}) async-start(bf16[128,20,128]{0,2,1:T(8,128)(2,1)} %bitcast.68), calls=%async_computation | async-start | bytes 1310720 | tf_op jit(solution)/shard_map/all_to_all | solution.py:63
  73.5 21.1 %all-to-all-start.6 = ((bf16[128,20,128]{0,2,1:T(8,128)(2,1)}), bf16[128,20,128]{0,2,1:T(8,128)(2,1)S(1)}, u32[]{:S(2)}, u32[]{:S(2)}) async-start(bf16[128,20,128]{0,2,1:T(8,128)(2,1)} %bitcast.66), calls=%async_computation.6 | async-start | bytes 1310720 | tf_op jit(solution)/shard_map/all_to_all | solution.py:84
  79.8 5.8 %copy-start.5 = (bf16[4,128,5,128]{3,1,0,2:T(8,128)(2,1)}, bf16[4,128,5,128]{3,1,0,2:T(8,128)(2,1)S(1)}, u32[]{:S(2)}) copy-start(bf16[4,128,5,128]{3,1,0,2:T(8,128)(2,1)S(1)} %copy.62) | copy-start | bytes 1966084
  81.5 16.6 %copy-start.3 = (bf16[4,128,5,128]{3,1,0,2:T(8,128)(2,1)}, bf16[4,128,5,128]{3,1,0,2:T(8,128)(2,1)S(1)}, u32[]{:S(2)}) copy-start(bf16[4,128,5,128]{3,1,0,2:T(8,128)(2,1)S(1)} %copy.68) | copy-start | bytes 1966084
  94.6 15.5 %all-to-all-start.4 = ((bf16[128,20,128]{0,2,1:T(8,128)(2,1)}), bf16[128,20,128]{0,2,1:T(8,128)(2,1)S(1)}, u32[]{:S(2)}, u32[]{:S(2)}) async-start(bf16[128,20,128]{0,2,1:T(8,128)(2,1)} %bitcast.20), calls=%async_computation.4 | async-start | bytes 1310720 | tf_op jit(solution)/shard_map/all_to_all | solution.py:94
  110.1 17.9 %all-to-all-start.3 = ((bf16[512,5,128]{2,1,0:T(8,128)(2,1)}), bf16[512,5,128]{2,1,0:T(8,128)(2,1)S(1)}, u32[]{:S(2)}, u32[]{:S(2)}) async-start(bf16[512,5,128]{2,1,0:T(8,128)(2,1)} %copy.70), calls=%async_computation.3 | async-start | bytes 2097152 | tf_op jit(solution)/shard_map/all_to_all | solution.py:105
  114.9 1.1 copy-start.8
  114.9 2.8 copy-start.11
  117.6 1.1 copy-start.6
  117.7 1.3 copy-start.7
  119.0 1.8 copy-start.4
  128.0 17.9 %all-to-all-start.7 = ((bf16[512,5,128]{2,1,0:T(8,128)(2,1)}), bf16[512,5,128]{2,1,0:T(8,128)(2,1)S(1)}, u32[]{:S(2)}, u32[]{:S(2)}) async-start(bf16[512,5,128]{2,1,0:T(8,128)(2,1)} %copy.84), calls=%async_computation.7 | async-start | bytes 2097152 | tf_op jit(solution)/shard_map/all_to_all | solution.py:106
Sparse Core Ops, SparseCore 0:
  15.6 297.6 all-gather.1
where the time goes:
time: 335 us; the launch traced here: 334 us
  waiting for transfers between devices  215 us (64%)
  blocking collectives  34.9 us (10%)
  matrix products  25 us (7%)
  starting transfers between devices  21.3 us (6%)
  local copies, waits for them, and re-layouts  19.5 us (6%)
  between operations  14.3 us (4%)
  other arithmetic  3.83 us (1%)
    all_gather x1, waiting for transfers between devices, body(): lax.all_gather(full_rows, 'dp', axis=1, tiled=True)  166 us
    all_to_all x1, waiting for transfers between devices, body(): lax.all_to_all(dual_attn, 'seq', split_axis=0, concat_axis=1, tiled=True)  13.8 us
    all_to_all x1, blocking collectives, body(): lax.all_to_all(query_dual.reshape(rows_here, HEADS, HDIM), 'seq', split_a...  13.4 us
    all_to_all x1, blocking collectives, body(): lax.all_to_all(value_states.reshape(rows_here, HEADS, HDIM), 'seq', split...  13.3 us
    dot_general x1, matrix products, body(): jnp.dot(stacked, lax.all_gather(full_rows, 'dp', axis=1, tiled=True), pre...  12.3 us
    all_to_all x1, waiting for transfers between devices, body(): lax.all_to_all(key_dual.reshape(rows_here, HEADS, HDIM), 'seq', split_axi...  8.99 us
    all_to_all x1, waiting for transfers between devices, body(): lax.all_to_all(query_normed.reshape(rows_here, HEADS, HDIM), 'seq', split...  8.77 us
    all_gather x1, blocking collectives, body(): full_rows = lax.all_gather(out_weight, 'seq', axis=0, tiled=True)  8.24 us
  transfers between devices with their start and end apart: 7, of which 7 were waited for; matrix products, arithmetic and copies ran while one was open for 10% of the time, Pallas kernels for 0%

commit v1 on v0

--- a/solution.py
+++ b/solution.py
@@ -5,6 +5,11 @@
 
 HEADS = 20
 HDIM = 128
+
+
+def exchange_gather(value, mesh_axis, along):
+    sent = jnp.stack([value] * lax.axis_size(mesh_axis))
+    return jnp.concatenate(lax.all_to_all(sent, mesh_axis, 0, 0), axis=along)
 
 
 def rms_tangent(primal, tangent, gain):
@@ -110,9 +115,7 @@
     )
     full_rows = lax.all_gather(out_weight, "seq", axis=0, tiled=True)
     result = jnp.dot(
-        stacked,
-        lax.all_gather(full_rows, "dp", axis=1, tiled=True),
-        preferred_element_type=jnp.float32,
+        stacked, exchange_gather(full_rows, "dp", 1), preferred_element_type=jnp.float32
     ).astype(jnp.bfloat16)
     return (result[:rows_here], result[rows_here:])
 

time: 335 us -> 844 us (2.52)
  the two profiles are of different devices: /device:TPU:24 before, /device:TPU:248 now
where the time goes in v1:
time: 844 us; the launch traced here: 843 us
  waiting for transfers between devices  710 us (84%)
  starting transfers between devices  36.3 us (4%)
  matrix products  33.1 us (4%)
  blocking collectives  30 us (4%)
  local copies, waits for them, and re-layouts  28 us (3%)
    all_to_all x1, waiting for transfers between devices, exchange_gather(): return jnp.concatenate(lax.all_to_all(sent, mesh_axis, 0, 0), axis=along)  671 us
    all_gather x1, blocking collectives, body(): full_rows = lax.all_gather(out_weight, 'seq', axis=0, tiled=True)  17.4 us
  transfers between devices with their start and end apart: 8, of which 6 were waited for; matrix products, arithmetic and copies ran while one was open for 3% of the time, Pallas kernels for 0%

profile of v1, /device:TPU:248, one launch (start us, length us, event | category | flops | bytes accessed | tf_op | source)
XLA Modules:
  0.0 842.7 jit_solution(5476868527706338523)
XLA Ops:
  0.6 2.3 copy.74
  2.9 3.5 all-to-all-start.4
  6.4 0.3 copy.78
  6.8 0.3 copy.61
  7.1 1.4 copy.81
  8.5 1.4 copy.64
  9.9 0.4 fusion.19
  10.4 0.4 fusion.24
  10.8 1.6 fusion.11
  12.4 4.2 all-to-all-done.4
  16.6 3.5 all-to-all-start
  20.1 1.6 fusion.14
  21.7 8.6 %all-to-all-done = bf16[128,20,128]{0,2,1:T(8,128)(2,1)S(1)} async-done(((bf16[128,20,128]{0,2,1:T(8,128)(2,1)}), bf16[128,20,128]{0,2,1:T(8,128)(2,1)S(1)}, u32[]{:S(2)}, u32[]{:S(2)}) %all-to-all-start) | async-done | bytes 655392 | tf_op jit(solution)/shard_map/all_to_all | solution.py:68
  30.3 3.5 all-to-all-start.1
  33.8 1.4 copy.67
  35.2 8.8 %all-to-all-done.1 = bf16[128,20,128]{0,2,1:T(8,128)(2,1)S(1)} async-done(((bf16[128,20,128]{0,2,1:T(8,128)(2,1)}), bf16[128,20,128]{0,2,1:T(8,128)(2,1)S(1)}, u32[]{:S(2)}, u32[]{:S(2)}) %all-to-all-start.1) | async-done | bytes 655392 | tf_op jit(solution)/shard_map/all_to_all | solution.py:82
  43.9 12.6 %all_to_all.143 = bf16[128,20,128]{0,2,1:T(8,128)(2,1)S(1)} all-to-all(bf16[128,20,128]{0,2,1:T(8,128)(2,1)S(1)} %bitcast.70), channel_id=1, replica_groups=mesh['dp'=64,'seq'=4] {'seq'}, dimensions={1} | all-to-all | bytes 1310720 | tf_op jit(solution)/shard_map/all_to_all | solution.py:92
  56.6 3.5 all-to-all-start.5
  60.0 1.1 copy.63
  61.1 0.3 copy.66
  61.5 8.7 %all-to-all-done.5 = bf16[128,20,128]{0,2,1:T(8,128)(2,1)S(1)} async-done(((bf16[128,20,128]{0,2,1:T(8,128)(2,1)}), bf16[128,20,128]{0,2,1:T(8,128)(2,1)S(1)}, u32[]{:S(2)}, u32[]{:S(2)}) %all-to-all-start.5) | async-done | bytes 655392 | tf_op jit(solution)/shard_map/all_to_all | solution.py:75
  70.2 3.7 all-to-all-start.6
  73.9 5.2 fusion.40
  79.1 1.1 copy.76
  80.1 1.1 copy.69
  81.2 0.3 copy.80
  81.6 3.2 fusion.41
  84.8 1.1 copy.83
  85.9 3.8 fusion.28
  89.7 0.1 slice-done.1
  89.8 0.1 copy-done.2
  90.0 0.2 copy-done.4
  90.2 3.8 multiply_reduce_fusion
  94.1 1.3 fusion.31
  95.4 1.4 copy.85
  96.8 3.5 all-to-all-start.7
  100.3 3.5 fusion.32
  103.9 1.4 copy.71
  105.3 9.4 %all-to-all-done.7 = bf16[512,5,128]{2,1,0:T(8,128)(2,1)S(1)} async-done(((bf16[512,5,128]{2,1,0:T(8,128)(2,1)}), bf16[512,5,128]{2,1,0:T(8,128)(2,1)S(1)}, u32[]{:S(2)}, u32[]{:S(2)}) %all-to-all-start.7) | async-done | bytes 655392 | tf_op jit(solution)/shard_map/all_to_all | solution.py:111
  114.7 3.5 all-to-all-start.3
  118.3 17.4 %all_gather.3 = bf16[2560,80]{0,1:T(8,128)(2,1)S(1)} all-gather(bf16[640,80]{0,1:T(8,128)(2,1)S(1)} %copy-done.5), channel_id=1, replica_groups=mesh['dp'=64,'seq'=4] {'seq'}, dimensions={0}, use_global_device_ids=true | all-gather | bytes 512000 | tf_op jit(solution)/shard_map/all_gather | solution.py:116
  135.7 8.8 %stack.2 = bf16[64,2560,80]{1,2,0:T(8,128)(2,1)} broadcast(bf16[2560,80]{0,1:T(8,128)(2,1)S(1)} %all_gather.3), dimensions={1,2} | broadcast | bytes 26624000 | tf_op jit(solution)/shard_map/stack | solution.py:11
  144.5 11.6 %all-to-all-start.8 = ((bf16[64,2560,80]{1,2,0:T(8,128)(2,1)}), bf16[64,2560,80]{1,2,0:T(8,128)(2,1)}, u32[]{:S(2)}, u32[]{:S(2)}) async-start(bf16[64,2560,80]{1,2,0:T(8,128)(2,1)} %stack.2), calls=%async_computation.8 | async-start | bytes 52428800 | tf_op jit(solution)/shard_map/all_to_all | solution.py:12
  156.2 0.6 copy.87
  156.8 1.3 copy.73
  158.1 670.6 %all-to-all-done.8 = bf16[64,2560,80]{1,2,0:T(8,128)(2,1)} async-done(((bf16[64,2560,80]{1,2,0:T(8,128)(2,1)}), bf16[64,2560,80]{1,2,0:T(8,128)(2,1)}, u32[]{:S(2)}, u32[]{:S(2)}) %all-to-all-start.8) | async-done | bytes 26214432 | tf_op jit(solution)/shard_map/all_to_all | solution.py:12
  828.8 12.3 %convolution_convert_fusion = bf16[256,5120]{1,0:T(8,128)(2,1)S(1)} fusion(bf16[2560,5120]{0,1:T(8,128)(2,1)} %bitcast.41, bf16[128,2560]{0,1:T(8,128)(2,1)S(1)} %bitcast.80, bf16[128,2560]{0,1:T(8,128)(2,1)} %bitcast.82), kind=kOutput, calls=%fused_computation.1 | convolution fusion | flops 6714818560 | bytes 30146560 | tf_op jit(solution)/shard_map/dot_general | solution.py:117
  841.0 1.7 fusion.39
  (27 shorter events, 0.1 us)
Async XLA Ops:
  0.6 5.8 copy-start
  0.6 6.1 copy-start.1
  2.9 13.7 %all-to-all-start.4 = ((bf16[128,20,128]{0,2,1:T(8,128)(2,1)}), bf16[128,20,128]{0,2,1:T(8,128)(2,1)S(1)}, u32[]{:S(2)}, u32[]{:S(2)}) async-start(bf16[128,20,128]{0,2,1:T(8,128)(2,1)} %bitcast.20), calls=%async_computation.4 | async-start | bytes 1310720 | tf_op jit(solution)/shard_map/all_to_all | solution.py:99
  7.1 3.7 copy-start.6
  10.3 9.7 %copy-start.7 = (f32[2560]{0:T(1024)S(1)}, f32[2560]{0:T(1024)}, u32[]{:S(2)}) copy-start(f32[2560]{0:T(1024)} %param.16) | copy-start | bytes 30724
  16.6 13.7 %all-to-all-start = ((bf16[128,20,128]{0,2,1:T(8,128)(2,1)}), bf16[128,20,128]{0,2,1:T(8,128)(2,1)S(1)}, u32[]{:S(2)}, u32[]{:S(2)}) async-start(bf16[128,20,128]{0,2,1:T(8,128)(2,1)} %bitcast.73), calls=%async_computation | async-start | bytes 1310720 | tf_op jit(solution)/shard_map/all_to_all | solution.py:68
  30.3 13.7 %all-to-all-start.1 = ((bf16[128,20,128]{0,2,1:T(8,128)(2,1)}), bf16[128,20,128]{0,2,1:T(8,128)(2,1)S(1)}, u32[]{:S(2)}, u32[]{:S(2)}) async-start(bf16[128,20,128]{0,2,1:T(8,128)(2,1)} %bitcast.74), calls=%async_computation.1 | async-start | bytes 1310720 | tf_op jit(solution)/shard_map/all_to_all | solution.py:82
  56.6 13.7 %all-to-all-start.5 = ((bf16[128,20,128]{0,2,1:T(8,128)(2,1)}), bf16[128,20,128]{0,2,1:T(8,128)(2,1)S(1)}, u32[]{:S(2)}, u32[]{:S(2)}) async-start(bf16[128,20,128]{0,2,1:T(8,128)(2,1)} %bitcast.72), calls=%async_computation.5 | async-start | bytes 1310720 | tf_op jit(solution)/shard_map/all_to_all | solution.py:75
  70.2 14.5 %all-to-all-start.6 = ((bf16[128,20,128]{0,2,1:T(8,128)(2,1)}), bf16[128,20,128]{0,2,1:T(8,128)(2,1)S(1)}, u32[]{:S(2)}, u32[]{:S(2)}) async-start(bf16[128,20,128]{0,2,1:T(8,128)(2,1)} %bitcast.71), calls=%async_computation.6 | async-start | bytes 1310720 | tf_op jit(solution)/shard_map/all_to_all | solution.py:89
  84.8 4.9 slice-start
  85.9 4.0 slice-start.1
  85.9 4.1 copy-start.2
  85.9 4.3 copy-start.4
  85.9 8.2 slice-start.2
  90.2 3.9 copy-start.3
  90.2 3.9 slice-start.3
  96.8 17.9 %all-to-all-start.7 = ((bf16[512,5,128]{2,1,0:T(8,128)(2,1)}), bf16[512,5,128]{2,1,0:T(8,128)(2,1)S(1)}, u32[]{:S(2)}, u32[]{:S(2)}) async-start(bf16[512,5,128]{2,1,0:T(8,128)(2,1)} %copy.85), calls=%async_computation.7 | async-start | bytes 2097152 | tf_op jit(solution)/shard_map/all_to_all | solution.py:111
  103.9 14.4 %copy-start.5 = (bf16[640,80]{0,1:T(8,128)(2,1)S(1)}, bf16[640,80]{0,1:T(8,128)(2,1)}, u32[]{:S(2)}) copy-start(bf16[640,80]{0,1:T(8,128)(2,1)} %param.17) | copy-start | bytes 307204
  114.7 21.0 %all-to-all-start.3 = ((bf16[512,5,128]{2,1,0:T(8,128)(2,1)}), bf16[512,5,128]{2,1,0:T(8,128)(2,1)S(1)}, u32[]{:S(2)}, u32[]{:S(2)}) async-start(bf16[512,5,128]{2,1,0:T(8,128)(2,1)} %copy.71), calls=%async_computation.3 | async-start | bytes 2097152 | tf_op jit(solution)/shard_map/all_to_all | solution.py:110
  144.5 684.2 %all-to-all-start.8 = ((bf16[64,2560,80]{1,2,0:T(8,128)(2,1)}), bf16[64,2560,80]{1,2,0:T(8,128)(2,1)}, u32[]{:S(2)}, u32[]{:S(2)}) async-start(bf16[64,2560,80]{1,2,0:T(8,128)(2,1)} %stack.2), calls=%async_computation.8 | async-start | bytes 52428800 | tf_op jit(solution)/shard_map/all_to_all | solution.py:12
